TPU v7x, 32 devices: a whole 2x2x4 slice. The times are simulated.
32 devices in a mesh: node: 4 (over y, core), edge: 8 (over z, x).
Axes of the slice: x: 2, y: 2, z: 4, core: 2. Of those that a mesh axis runs over, the one named last changes fastest.
Arguments:
- atoms: bfloat16 [4096, 1152], P(('node', 'edge')), may hold values from -6 to 6
- cotangent: bfloat16 [4096, 1152], P(('node', 'edge')), may hold values from -6 to 6
- params: float32 [409600], P('node'), may hold values from -4 to 4
- adam_m: float32 [409600], P('node'), may hold values from -4 to 4
- adam_v: float32 [409600], P('node'), may hold values from 0.3 to 3
- sends: int32 [4, 8, 128], P('node', 'edge'), may hold values from 0 to 127
- edge_slot: int32 [4096, 4], P(('node', 'edge')), may hold values from 0 to 127
- rot_index: int32 [4096, 4], P(('node', 'edge')), may hold values from 0 to 63
- rot_table: float32 [64, 9, 9], replicated, may hold values from -1.2 to 2, as said below
- edge_gain: float32 [4096, 4], P(('node', 'edge')), may hold values from 0.3 to 3
- live_tiles: int32 [4, 8], P('node', 'edge'), may hold values from 1 to 4, as said below
Outputs:
- output: bfloat16 [4096, 1152], P(('node', 'edge'))
- grad_atoms: bfloat16 [4096, 1152], P(('node', 'edge'))
- new_params: float32 [409600], P('node')
- new_moment_one: float32 [409600], P('node')
- new_moment_two: float32 [409600], P('node')
Inputs may be any that keep to these rules, and one draw needn't show every extreme that they name: The first live_tiles[n, e] edge tiles of a device are live; some device has all 4 tiles live. `rot_table`: rotations of degrees 0, 1 and 2 act on harmonics 0, 1 to 3 and 4 to 8 only.
All inputs are finite; a program needn't handle non-finite values.
Results may differ from a plain program's by a relative error of at most 0.0015.
The roundings to bfloat16 on the way count: a program that leaves them out, or rounds other values in their place, can miss the bound.
Values may be sent and summed in bfloat16 or wider, within the bound.
No kernel may reach another device: no remote copies, remote signals or barrier semaphores. Data moves between devices by JAX's collectives and lax.ppermute only.
A program may use at most 64 MiB of HBM per device.

v0:
```python
import jax
import jax.numpy as jnp
from jax import lax
from jax.sharding import PartitionSpec as P

C = 128
HARM = 9
FFH = 256
K = 4
TILE_ATOMS = 32
ROTS = 64
harmonic_order = (0, 2, 6, 3, 7, 1, 5, 8, 4)
highest = lax.Precision.HIGHEST
norm_epsilon = 1e-06
first_beta = 0.8
second_beta = 0.95
step_count = 100
learn_rate = 0.01
decay_rate = 0.01
adam_epsilon = 1e-08
grad_boost = 4.0


def unpack_weights(weights):
    lengths = [9 * C * C, 4 * C * C, 4 * C * C, C * C, C * C, C * FFH, C * FFH, FFH * C]
    starts = [0]
    for length in lengths:
        starts.append(starts[-1] + length)

    def take_piece(number, shape_pair):
        return weights[starts[number] : starts[number + 1]].reshape(shape_pair)

    zero_weight = take_piece(0, (3 * C, 3 * C))
    one_real = take_piece(1, (2 * C, 2 * C))
    one_imag = take_piece(2, (2 * C, 2 * C))
    two_real = take_piece(3, (C, C))
    two_imag = take_piece(4, (C, C))
    gate_weight = take_piece(5, (C, FFH))
    up_weight = take_piece(6, (C, FFH))
    down_weight = take_piece(7, (FFH, C))
    one_block = jnp.concatenate(
        [
            jnp.concatenate([one_real, one_imag], axis=1),
            jnp.concatenate([-one_imag, one_real], axis=1),
        ],
        axis=0,
    )
    two_block = jnp.concatenate(
        [
            jnp.concatenate([two_real, two_imag], axis=1),
            jnp.concatenate([-two_imag, two_real], axis=1),
        ],
        axis=0,
    )
    return (zero_weight, one_block, two_block, gate_weight, up_weight, down_weight)


def edge_forward(sources, rotation, edge_gains, matrices):
    zero_weight, one_block, two_block = (matrices[0], matrices[1], matrices[2])
    total_edges = sources.shape[0]
    rotated = jnp.einsum(
        "eij,ejc->eic", rotation, sources.astype(jnp.float32), precision=highest
    ).astype(jnp.bfloat16)
    zero_part = jnp.dot(
        rotated[:, 0:3].reshape(total_edges, 3 * C), zero_weight, preferred_element_type=jnp.float32
    ) * (3 * C) ** (-0.5)
    one_part = jnp.dot(
        rotated[:, 3:7].reshape(total_edges, 4 * C), one_block, preferred_element_type=jnp.float32
    ) * (4 * C) ** (-0.5)
    two_part = jnp.dot(
        rotated[:, 7:9].reshape(total_edges, 2 * C), two_block, preferred_element_type=jnp.float32
    ) * (2 * C) ** (-0.5)
    mixed = (
        jnp.concatenate([zero_part, one_part, two_part], axis=1).reshape(total_edges, HARM, C)
        * edge_gains[:, None, None]
    )
    messages = jnp.einsum("eji,ejc->eic", rotation, mixed, precision=highest)
    return (rotated, messages)


def edge_backward(rotated, rotation, edge_gains, upstream, matrices):
    zero_weight, one_block, two_block = (matrices[0], matrices[1], matrices[2])
    total_edges = rotated.shape[0]
    grad_mixed = (
        jnp.einsum("eij,ejc->eic", rotation, upstream, precision=highest)
        * edge_gains[:, None, None]
    ).astype(jnp.bfloat16)
    zero_in = rotated[:, 0:3].reshape(total_edges, 3 * C)
    one_in = rotated[:, 3:7].reshape(total_edges, 4 * C)
    two_in = rotated[:, 7:9].reshape(total_edges, 2 * C)
    zero_out = grad_mixed[:, 0:3].reshape(total_edges, 3 * C)
    one_out = grad_mixed[:, 3:7].reshape(total_edges, 4 * C)
    two_out = grad_mixed[:, 7:9].reshape(total_edges, 2 * C)
    zero_grad = jnp.dot(zero_in.T, zero_out, preferred_element_type=jnp.float32) * (3 * C) ** (-0.5)
    one_grad = jnp.dot(one_in.T, one_out, preferred_element_type=jnp.float32) * (4 * C) ** (-0.5)
    two_grad = jnp.dot(two_in.T, two_out, preferred_element_type=jnp.float32) * (2 * C) ** (-0.5)
    back_zero = jnp.dot(zero_out, zero_weight.T, preferred_element_type=jnp.float32) * (3 * C) ** (
        -0.5
    )
    back_one = jnp.dot(one_out, one_block.T, preferred_element_type=jnp.float32) * (4 * C) ** (-0.5)
    back_two = jnp.dot(two_out, two_block.T, preferred_element_type=jnp.float32) * (2 * C) ** (-0.5)
    grad_rotated = jnp.concatenate([back_zero, back_one, back_two], axis=1).reshape(
        total_edges, HARM, C
    )
    grad_sources = jnp.einsum("eij,eic->ejc", rotation, grad_rotated, precision=highest)
    return (grad_sources, (zero_grad, one_grad, two_grad))


def ffn_forward(atoms_block, aggregate, matrices):
    gate_weight, up_weight, down_weight = (matrices[3], matrices[4], matrices[5])
    number = atoms_block.shape[0]
    height = atoms_block.astype(jnp.float32).reshape(number, HARM, C) + aggregate
    inverse = lax.rsqrt(jnp.mean(height * height, axis=(1, 2), keepdims=True) + norm_epsilon)
    normed = height * inverse
    normed_low = normed.astype(jnp.bfloat16)
    gate_value = jax.nn.sigmoid(
        jnp.dot(normed_low[:, 0, :], gate_weight, preferred_element_type=jnp.float32) * C ** (-0.5)
    )
    up_value = jnp.dot(
        normed_low.reshape(number * HARM, C), up_weight, preferred_element_type=jnp.float32
    ).reshape(number, HARM, FFH) * C ** (-0.5)
    hidden_low = (up_value * gate_value[:, None, :]).astype(jnp.bfloat16)
    projected = jnp.dot(
        hidden_low.reshape(number * HARM, FFH), down_weight, preferred_element_type=jnp.float32
    ).reshape(number, HARM, C)
    output = (height + projected * FFH ** (-0.5)).astype(jnp.bfloat16)
    return (output, (inverse, normed, normed_low, gate_value, up_value, hidden_low))


def ffn_backward(stored, cotangent, matrices):
    gate_weight, up_weight, down_weight = (matrices[3], matrices[4], matrices[5])
    inverse, normed, normed_low, gate_value, up_value, hidden_low = stored
    number = cotangent.shape[0]
    upstream = cotangent.reshape(number * HARM, C)
    down_grad = jnp.dot(
        hidden_low.reshape(number * HARM, FFH).T, upstream, preferred_element_type=jnp.float32
    ) * FFH ** (-0.5)
    grad_hidden = jnp.dot(upstream, down_weight.T, preferred_element_type=jnp.float32).reshape(
        number, HARM, FFH
    ) * FFH ** (-0.5)
    grad_up = (grad_hidden * gate_value[:, None, :]).astype(jnp.bfloat16)
    grad_gate = (jnp.sum(grad_hidden * up_value, axis=1) * gate_value * (1.0 - gate_value)).astype(
        jnp.bfloat16
    )
    up_grad = jnp.dot(
        normed_low.reshape(number * HARM, C).T,
        grad_up.reshape(number * HARM, FFH),
        preferred_element_type=jnp.float32,
    ) * C ** (-0.5)
    gate_grad = jnp.dot(
        normed_low[:, 0, :].T, grad_gate, preferred_element_type=jnp.float32
    ) * C ** (-0.5)
    grad_normed = jnp.dot(
        grad_up.reshape(number * HARM, FFH), up_weight.T, preferred_element_type=jnp.float32
    ).reshape(number, HARM, C) * C ** (-0.5)
    grad_normed = grad_normed.at[:, 0, :].add(
        jnp.dot(grad_gate, gate_weight.T, preferred_element_type=jnp.float32) * C ** (-0.5)
    )
    grad_height = cotangent.astype(jnp.float32).reshape(number, HARM, C) + inverse * (
        grad_normed - normed * jnp.mean(grad_normed * normed, axis=(1, 2), keepdims=True)
    )
    return (grad_height, (gate_grad, up_grad, down_grad))


def flat_grads(zero_grad, one_grad, two_grad, gate_grad, up_grad, down_grad):
    half_one = 2 * C
    one_real = one_grad[:half_one, :half_one] + one_grad[half_one:, half_one:]
    one_imag = one_grad[:half_one, half_one:] - one_grad[half_one:, :half_one]
    two_real = two_grad[:C, :C] + two_grad[C:, C:]
    two_imag = two_grad[:C, C:] - two_grad[C:, :C]
    pieces = [zero_grad, one_real, one_imag, two_real, two_imag, gate_grad, up_grad, down_grad]
    return jnp.concatenate([matrix.reshape(-1) for matrix in pieces])


def adam_step(params, moment_one, moment_two, gradient):
    new_one = first_beta * moment_one + (1.0 - first_beta) * gradient
    new_two = second_beta * moment_two + (1.0 - second_beta) * gradient * gradient
    corrected = (
        new_one
        / (1.0 - first_beta**step_count)
        / (jnp.sqrt(new_two / (1.0 - second_beta**step_count)) + adam_epsilon)
    )
    return (params - learn_rate * (corrected + decay_rate * params), new_one, new_two)


def shards(
    atoms,
    cotangent,
    params,
    adam_m,
    adam_v,
    sends,
    edge_slot,
    rot_index,
    rot_table,
    edge_gain,
    live_tiles,
):
    node_size = lax.axis_size("node")
    edge_size = lax.axis_size("edge")
    weights = lax.all_gather(params.astype(jnp.bfloat16), "node", axis=0, tiled=True)
    matrices = unpack_weights(weights)
    rot_rows = rot_table[:, jnp.array(harmonic_order, dtype=jnp.int32), :].reshape(
        ROTS, HARM * HARM
    )
    outgoing = sends.reshape(-1)
    local_atoms = atoms.shape[0]
    features = atoms.shape[1]
    slot_count = outgoing.shape[0]
    per_peer = slot_count // edge_size
    wanted = lax.all_to_all(
        outgoing.reshape(edge_size, per_peer), "edge", split_axis=0, concat_axis=0, tiled=True
    )
    blocks = lax.all_gather(atoms, "edge", axis=0, tiled=True)
    offsets = jnp.arange(edge_size, dtype=jnp.int32)[:, None] * local_atoms
    slot_rows = blocks[(wanted + offsets).reshape(-1)]
    tile_edges = TILE_ATOMS * K
    live_count = live_tiles.reshape(-1)[0]
    edge_total = local_atoms * K
    slots_flat = edge_slot.reshape(-1)
    index_flat = rot_index.reshape(-1)
    gains_flat = edge_gain.reshape(-1)
    rot_range = jnp.arange(ROTS, dtype=jnp.int32)

    def tile_inputs(tile_number):
        first_edge = tile_number * tile_edges
        slots_here = lax.dynamic_slice_in_dim(slots_flat, first_edge, tile_edges)
        index_here = lax.dynamic_slice_in_dim(index_flat, first_edge, tile_edges)
        gains_here = lax.dynamic_slice_in_dim(gains_flat, first_edge, tile_edges)
        onehot = (index_here[:, None] == rot_range[None, :]).astype(jnp.float32)
        rotation = jnp.dot(onehot, rot_rows, precision=highest).reshape(tile_edges, HARM, HARM)
        return (slots_here, rotation, gains_here)

    def forward_tile(tile_number, loop_state):
        aggregate, rotated_all = loop_state
        slots_here, rotation, gains_here = tile_inputs(tile_number)
        sources = slot_rows[slots_here].reshape(tile_edges, HARM, C)
        rotated, messages = edge_forward(sources, rotation, gains_here, matrices)
        summed = messages.reshape(TILE_ATOMS, K, HARM, C).sum(axis=1) * K ** (-0.5)
        aggregate = lax.dynamic_update_slice_in_dim(aggregate, summed, tile_number * TILE_ATOMS, 0)
        rotated_all = lax.dynamic_update_slice_in_dim(
            rotated_all, rotated, tile_number * tile_edges, 0
        )
        return (aggregate, rotated_all)

    empty_state = (
        jnp.zeros((local_atoms, HARM, C), jnp.float32),
        jnp.zeros((edge_total, HARM, C), jnp.bfloat16),
    )
    aggregate, rotated_all = lax.fori_loop(0, live_count, forward_tile, empty_state)
    output, stored = ffn_forward(atoms, aggregate, matrices)
    grad_height, ffn_grads = ffn_backward(stored, cotangent, matrices)

    def backward_tile(tile_number, loop_state):
        slot_grad, zero_acc, one_acc, two_acc = loop_state
        slots_here, rotation, gains_here = tile_inputs(tile_number)
        rotated = lax.dynamic_slice_in_dim(rotated_all, tile_number * tile_edges, tile_edges, 0)
        height_here = lax.dynamic_slice_in_dim(grad_height, tile_number * TILE_ATOMS, TILE_ATOMS, 0)
        upstream = jnp.broadcast_to(height_here[:, None], (TILE_ATOMS, K, HARM, C)).reshape(
            tile_edges, HARM, C
        ) * K ** (-0.5)
        grad_sources, weight_parts = edge_backward(
            rotated, rotation, gains_here, upstream, matrices
        )
        slot_grad = slot_grad.at[slots_here].add(grad_sources.reshape(tile_edges, HARM * C))
        return (
            slot_grad,
            zero_acc + weight_parts[0],
            one_acc + weight_parts[1],
            two_acc + weight_parts[2],
        )

    initial = (
        jnp.zeros((slot_count, features), jnp.float32),
        jnp.zeros((3 * C, 3 * C), jnp.float32),
        jnp.zeros((4 * C, 4 * C), jnp.float32),
        jnp.zeros((2 * C, 2 * C), jnp.float32),
    )
    slot_grad, zero_grad, one_grad, two_grad = lax.fori_loop(0, live_count, backward_tile, initial)
    returned = lax.all_to_all(
        slot_grad.reshape(edge_size, per_peer, features),
        "edge",
        split_axis=0,
        concat_axis=0,
        tiled=True,
    ).reshape(slot_count, features)
    gathered_back = jnp.zeros((local_atoms, features), jnp.float32).at[outgoing].add(returned)
    grad_atoms = (grad_height.reshape(local_atoms, features) + gathered_back).astype(jnp.bfloat16)
    all_atoms = local_atoms * node_size * edge_size
    gradient = flat_grads(
        zero_grad, one_grad, two_grad, ffn_grads[0], ffn_grads[1], ffn_grads[2]
    ) * (grad_boost * all_atoms ** (-0.5))
    partial_rows = lax.psum_scatter(
        gradient.astype(jnp.bfloat16), "node", scatter_dimension=0, tiled=True
    )
    own_grad = lax.psum(partial_rows, "edge").astype(jnp.float32)
    new_params, new_one, new_two = adam_step(params, adam_m, adam_v, own_grad)
    return (output.reshape(local_atoms, features), grad_atoms, new_params, new_one, new_two)


def solution(mesh):
    return jax.shard_map(
        shards,
        mesh=mesh,
        in_specs=(
            P(("node", "edge"), None),
            P(("node", "edge"), None),
            P("node"),
            P("node"),
            P("node"),
            P("node", "edge", None),
            P(("node", "edge"), None),
            P(("node", "edge"), None),
            P(),
            P(("node", "edge"), None),
            P("node", "edge"),
        ),
        out_specs=(
            P(("node", "edge"), None),
            P(("node", "edge"), None),
            P("node"),
            P("node"),
            P("node"),
        ),
        check_vma=False,
    )
```

profile of v0, /device:TPU:0, one launch (start us, length us, event | category | flops | bytes accessed | tf_op | source)
XLA Modules:
  0.0 379.7 jit_solution(16567656678296600095)
XLA Ops:
  10.5 7.3 %all-to-all-start = ((s32[8,1,16]{2,1,0:T(1,128)}), s32[8,1,16]{2,1,0:T(1,128)S(1)}, u32[]{:S(2)}, u32[]{:S(2)}) async-start(s32[8,1,16]{2,1,0:T(1,128)} %bitcast.3), calls=%async_computation | async-start | bytes 8192 | tf_op jit(solution)/shard_map/all_to_all | solution.py:211
  17.8 2.0 copy.104
  22.3 8.8 %all_gather.7 = bf16[409600]{0:T(1024)(128)(2,1)S(1)} all-gather(bf16[102400]{0:T(1024)(128)(2,1)S(1)} %convert_element_type.38), channel_id=1, replica_groups=mesh['node'=4,'edge'=8] {'node'}, dimensions={0}, use_global_device_ids=true | all-gather | bytes 1024000 | tf_op jit(solution)/shard_map/all_gather | solution.py:201
  37.6 27.0 %all-gather.2.cloned.1.call-done = bf16[1024,1152]{1,0:T(8,128)(2,1)} async-done(((bf16[128,1152]{1,0:T(8,128)(2,1)}), bf16[1024,1152]{1,0:T(8,128)(2,1)}) %all-gather.2.cloned.1.call-update) | async-done | bytes 2359312 | tf_op jit(solution)/shard_map/all_gather | solution.py:214
  64.6 3.1 gather_fusion.2
  69.9 68.9 %while.31 = (s32[]{:T(128)}, f32[128,9,128]{2,1,0:T(8,128)}, bf16[512,9,128]{0,2,1:T(8,128)(2,1)}, s32[]{:T(128)}, s32[512]{0:T(512)S(1)}, /*index=5*/f32[64,81]...) while((s32[]{:T(128)}, f32[128,9,128]{2,1,0:T(8,128)}, ...), condition=%wide.region_2.0_spmd.clone, body=%wide.region_0.0_spmd.clone.sunk | while | flops 162342272 | bytes 14705741 | solution.py:250
  80.4 1.9 broadcast_multiply_fusion.5
  97.4 1.9 broadcast_multiply_fusion.5
  114.5 1.9 broadcast_multiply_fusion.5
  131.6 1.9 broadcast_multiply_fusion.5
  150.8 97.3 %while.32 = (s32[]{:T(128)}, f32[128,1152]{1,0:T(8,128)}, f32[384,384]{1,0:T(8,128)}, f32[512,512]{1,0:T(8,128)}, f32[256,256]{1,0:T(8,128)}, /*index=5*/s32[]{:...) while((s32[]{:T(128)}, f32[128,1152]{1,0:T(8,128)}, ...), condition=%wide.region_8.9_spmd.clone, body=%wide.region_6.8_spmd.clone.sunk | while | flops 284963200 | bytes 33641452 | solution.py:279
  164.7 3.6 scatter_fusion
  170.8 2.6 fusion.151
  188.8 3.6 scatter_fusion
  194.9 2.6 fusion.151
  212.9 3.6 scatter_fusion
  219.0 2.6 fusion.151
  237.0 3.6 scatter_fusion
  243.1 2.6 fusion.151
  258.6 32.6 %all-reduce.6.cloned.1.call-done = bf16[409600]{0:T(1024)(128)(2,1)} async-done(((bf16[409600]{0:T(1024)(128)(2,1)}), bf16[409600]{0:T(1024)(128)(2,1)}) %all-reduce.6.cloned.1.call-update) | async-done | bytes 819216
  295.2 5.5 %all-to-all-start.1 = ((f32[8,16,1152]{2,1,0:T(8,128)}), f32[8,16,1152]{2,1,0:T(8,128)S(1)}, u32[]{:S(2)}, u32[]{:S(2)}) async-start(f32[8,16,1152]{2,1,0:T(8,128)} %bitcast.17), calls=%async_computation.1 | async-start | bytes 1179648 | tf_op jit(solution)/shard_map/all_to_all | solution.py:280
  300.7 67.6 %all-reduce.4.cloned.1.call-done = bf16[102400]{0:T(1024)(128)(2,1)} async-done(((bf16[102400]{0:T(1024)(128)(2,1)}), bf16[102400]{0:T(1024)(128)(2,1)}) %all-reduce.4.cloned.1.call-update) | async-done | bytes 204816 | tf_op jit(solution)/shard_map/psum | solution.py:296
  368.3 2.2 multiply_subtract_fusion
  370.5 2.0 scatter_fusion.1
  (478 shorter events, 165.8 us)
Async XLA Ops:
  7.2 26.3 %copy-start = (f32[64,9,9]{0,2,1:T(8,128)S(1)}, f32[64,9,9]{0,2,1:T(8,128)}, u32[]{:S(2)}) copy-start(f32[64,9,9]{0,2,1:T(8,128)} %param.26) | copy-start | bytes 62212
  7.2 13.7 %copy-start.27 = (bf16[128,1152]{1,0:T(8,128)(2,1)S(1)}, bf16[128,1152]{1,0:T(8,128)(2,1)}, u32[]{:S(2)}) copy-start(bf16[128,1152]{1,0:T(8,128)(2,1)} %param.19) | copy-start | bytes 884740
  7.2 14.8 %copy-start.34 = (s32[128,4]{0,1:T(4,128)S(1)}, s32[128,4]{0,1:T(4,128)}, u32[]{:S(2)}) copy-start(s32[128,4]{0,1:T(4,128)} %param.25) | copy-start | bytes 6148
  7.2 15.0 %copy-start.25 = (f32[102400]{0:T(1024)S(1)}, f32[102400]{0:T(1024)}, u32[]{:S(2)}) copy-start(f32[102400]{0:T(1024)} %param.20) | copy-start | bytes 1228804
  7.2 57.4 %all-gather.2.cloned.1.call-start = ((), (), s32[]{:S(2)}) async-start(), calls=%async_computation.2 | async-start | bytes 2654208 | tf_op jit(solution)/shard_map/all_gather | solution.py:214
  10.5 26.4 %all-to-all-start = ((s32[8,1,16]{2,1,0:T(1,128)}), s32[8,1,16]{2,1,0:T(1,128)S(1)}, u32[]{:S(2)}, u32[]{:S(2)}) async-start(s32[8,1,16]{2,1,0:T(1,128)} %bitcast.3), calls=%async_computation | async-start | bytes 8192 | tf_op jit(solution)/shard_map/all_to_all | solution.py:211
  17.7 273.4 %all-reduce.6.cloned.1.call-start = ((), (), s32[]{:S(2)}) async-start(), calls=%async_computation.4 | async-start | bytes 1638400
  20.9 11.1 %copy-start.23 = (bf16[128,1152]{0,1:T(8,128)(2,1)}, bf16[128,1152]{0,1:T(8,128)(2,1)S(1)}, u32[]{:S(2)}) copy-start(bf16[128,1152]{0,1:T(8,128)(2,1)S(1)} %copy.113) | copy-start | bytes 884740
  22.2 9.1 %copy-start.39 = (s32[9]{0:T(128)S(1)}, s32[9]{0:T(128)}, u32[]{:S(2)}) copy-start(s32[9]{0:T(128)} %constant.134) | copy-start | bytes 112
  151.7 8.0 %copy-start.1 = (bf16[512,512]{1,0:T(8,128)(2,1)}, bf16[512,512]{1,0:T(8,128)(2,1)S(1)}, u32[]{:S(2)}) copy-start(bf16[512,512]{1,0:T(8,128)(2,1)S(1)} %get-tuple-element.700) | copy-start | bytes 1572868 | tf_op jit(solution)/shard_map/while
  151.7 9.2 %copy-start.5 = (bf16[384,384]{1,0:T(8,128)(2,1)}, bf16[384,384]{1,0:T(8,128)(2,1)S(1)}, u32[]{:S(2)}) copy-start(bf16[384,384]{1,0:T(8,128)(2,1)S(1)} %get-tuple-element.699) | copy-start | bytes 884740 | tf_op jit(solution)/shard_map/while
  175.8 8.0 %copy-start.1 = (bf16[512,512]{1,0:T(8,128)(2,1)}, bf16[512,512]{1,0:T(8,128)(2,1)S(1)}, u32[]{:S(2)}) copy-start(bf16[512,512]{1,0:T(8,128)(2,1)S(1)} %get-tuple-element.700) | copy-start | bytes 1572868 | tf_op jit(solution)/shard_map/while
  175.8 9.2 %copy-start.5 = (bf16[384,384]{1,0:T(8,128)(2,1)}, bf16[384,384]{1,0:T(8,128)(2,1)S(1)}, u32[]{:S(2)}) copy-start(bf16[384,384]{1,0:T(8,128)(2,1)S(1)} %get-tuple-element.699) | copy-start | bytes 884740 | tf_op jit(solution)/shard_map/while
  199.9 8.0 %copy-start.1 = (bf16[512,512]{1,0:T(8,128)(2,1)}, bf16[512,512]{1,0:T(8,128)(2,1)S(1)}, u32[]{:S(2)}) copy-start(bf16[512,512]{1,0:T(8,128)(2,1)S(1)} %get-tuple-element.700) | copy-start | bytes 1572868 | tf_op jit(solution)/shard_map/while
  199.9 9.2 %copy-start.5 = (bf16[384,384]{1,0:T(8,128)(2,1)}, bf16[384,384]{1,0:T(8,128)(2,1)S(1)}, u32[]{:S(2)}) copy-start(bf16[384,384]{1,0:T(8,128)(2,1)S(1)} %get-tuple-element.699) | copy-start | bytes 884740 | tf_op jit(solution)/shard_map/while
  224.0 8.0 %copy-start.1 = (bf16[512,512]{1,0:T(8,128)(2,1)}, bf16[512,512]{1,0:T(8,128)(2,1)S(1)}, u32[]{:S(2)}) copy-start(bf16[512,512]{1,0:T(8,128)(2,1)S(1)} %get-tuple-element.700) | copy-start | bytes 1572868 | tf_op jit(solution)/shard_map/while
  224.0 9.2 %copy-start.5 = (bf16[384,384]{1,0:T(8,128)(2,1)}, bf16[384,384]{1,0:T(8,128)(2,1)S(1)}, u32[]{:S(2)}) copy-start(bf16[384,384]{1,0:T(8,128)(2,1)S(1)} %get-tuple-element.699) | copy-start | bytes 884740 | tf_op jit(solution)/shard_map/while
  256.2 36.6 %copy-start.15 = (f32[128,9,128]{0,2,1:T(8,128)S(1)}, f32[128,9,128]{0,2,1:T(8,128)}, u32[]{:S(2)}) copy-start(f32[128,9,128]{0,2,1:T(8,128)} %copy-done.14) | copy-start | bytes 1769476
  257.3 37.7 %copy-start.20 = (f32[128,9,128]{0,2,1:T(8,128)S(1)}, f32[128,9,128]{0,2,1:T(8,128)}, u32[]{:S(2)}) copy-start(f32[128,9,128]{0,2,1:T(8,128)} %copy-done.19) | copy-start | bytes 1769476
  257.3 111.0 %all-reduce.4.cloned.1.call-start = ((), (), s32[]{:S(2)}) async-start(), calls=%async_computation.3 | async-start | bytes 409600 | tf_op jit(solution)/shard_map/psum | solution.py:296
  294.0 74.3 %copy-start.26 = (f32[102400]{0:T(1024)S(1)}, f32[102400]{0:T(1024)}, u32[]{:S(2)}) copy-start(f32[102400]{0:T(1024)} %param.20) | copy-start | bytes 1228804
  294.0 74.3 %copy-start.31 = (f32[102400]{0:T(1024)S(1)}, f32[102400]{0:T(1024)}, u32[]{:S(2)}) copy-start(f32[102400]{0:T(1024)} %param.22) | copy-start | bytes 1228804
  294.0 74.3 %copy-start.32 = (f32[102400]{0:T(1024)S(1)}, f32[102400]{0:T(1024)}, u32[]{:S(2)}) copy-start(f32[102400]{0:T(1024)} %param.21) | copy-start | bytes 1228804
  295.2 75.3 %all-to-all-start.1 = ((f32[8,16,1152]{2,1,0:T(8,128)}), f32[8,16,1152]{2,1,0:T(8,128)S(1)}, u32[]{:S(2)}, u32[]{:S(2)}) async-start(f32[8,16,1152]{2,1,0:T(8,128)} %bitcast.17), calls=%async_computation.1 | async-start | bytes 1179648 | tf_op jit(solution)/shard_map/all_to_all | solution.py:280
  (71 other events, 225.9 us)
Sparse Core Ops, SparseCore 0:
  10.2 54.3 all-gather.1
  257.4 33.7 all-reduce.5
  295.1 73.1 all-reduce.3
where the time goes:
time: 382 us; the launch traced here: 380 us
  waiting for transfers between devices  128 us (34%)
  local copies, waits for them, and re-layouts  86.5 us (23%)
  matrix products  67.4 us (18%)
  other arithmetic  52.7 us (14%)
  between operations  15 us (4%)
  starting transfers between devices  12.9 us (3%)
  blocking collectives  8.8 us (2%)
  loops' own time  8.4 us (2%)
    psum x1, waiting for transfers between devices, shards(): own_grad = lax.psum(partial_rows, 'edge').astype(jnp.float32)  67.6 us
    unnamed x4, waiting for transfers between devices  33.3 us
    all_gather x1, waiting for transfers between devices, shards(): blocks = lax.all_gather(atoms, 'edge', axis=0, tiled=True)  27 us
    scatter-add x4, other arithmetic, backward_tile(): slot_grad.at[slots_here].add(grad_sources.reshape(tile_edges, HARM * C))  14.6 us
    dot_general x4, matrix products, edge_backward(): jnp.dot(one_in.T, one_out, preferred_element_type=jnp.float32)  10.3 us
    unnamed x71, local copies, waits for them, and re-layouts  9.29 us
    all_gather x1, blocking collectives, shards(): lax.all_gather(params.astype(jnp.bfloat16), 'node', axis=0, tiled=True)  8.8 us
    mul x4, other arithmetic, edge_forward(): jnp.concatenate([zero_part, one_part, two_part], axis=1)  7.73 us
  transfers between devices with their start and end apart: 5, of which 3 were waited for; matrix products, arithmetic and copies ran while one was open for 5% of the time, Pallas kernels for 0%

commit v1 on v0

--- a/solution.py
+++ b/solution.py
@@ -293,7 +293,7 @@
     partial_rows = lax.psum_scatter(
         gradient.astype(jnp.bfloat16), "node", scatter_dimension=0, tiled=True
     )
-    own_grad = lax.psum(partial_rows, "edge").astype(jnp.float32)
+    own_grad = jnp.sum(lax.all_gather(partial_rows, "edge"), axis=0).astype(jnp.float32)
     new_params, new_one, new_two = adam_step(params, adam_m, adam_v, own_grad)
     return (output.reshape(local_atoms, features), grad_atoms, new_params, new_one, new_two)
 

time: 382 us -> 357 us (0.935)
  waiting for transfers between devices: 128 us -> 100 us
    psum x1 -> x0, waiting for transfers between devices: 67.6 us -> none  [shards(): own_grad = lax.psum(partial_rows, 'edge').astype(jnp.float32)]
    all_gather x0 -> x1, waiting for transfers between devices: none -> 20.8 us  [shards(): lax.all_gather(partial_rows, 'edge')]
    all_to_all x1, waiting for transfers between devices: 0.01 us -> 19.1 us  [shards(): lax.all_to_all(slot_grad.reshape(edge_size, per_peer, features), 'edge',...]
  transfers between devices with their start and end apart: 5 -> 5, of which waited for: 3 -> 4; matrix products, arithmetic and copies ran while one was open for 5% -> 5% of each run, Pallas kernels for 0% -> 0%
where the time goes in v1:
time: 357 us; the launch traced here: 355 us
  waiting for transfers between devices  100 us (28%)
  local copies, waits for them, and re-layouts  88.7 us (25%)
  matrix products  67.5 us (19%)
  other arithmetic  52.9 us (15%)
  between operations  15 us (4%)
  starting transfers between devices  13.1 us (4%)
  blocking collectives  8.8 us (2%)
  loops' own time  8.4 us (2%)
    unnamed x4, waiting for transfers between devices  33.3 us
    all_gather x1, waiting for transfers between devices, shards(): blocks = lax.all_gather(atoms, 'edge', axis=0, tiled=True)  27 us
    all_gather x1, waiting for transfers between devices, shards(): lax.all_gather(partial_rows, 'edge')  20.8 us
    all_to_all x1, waiting for transfers between devices, shards(): lax.all_to_all(slot_grad.reshape(edge_size, per_peer, features), 'edge',...  19.1 us
    scatter-add x4, other arithmetic, backward_tile(): slot_grad.at[slots_here].add(grad_sources.reshape(tile_edges, HARM * C))  14.6 us
    dot_general x4, matrix products, edge_backward(): jnp.dot(one_in.T, one_out, preferred_element_type=jnp.float32)  10.3 us
    unnamed x71, local copies, waits for them, and re-layouts  9.39 us
    all_gather x1, blocking collectives, shards(): lax.all_gather(params.astype(jnp.bfloat16), 'node', axis=0, tiled=True)  8.8 us
  transfers between devices with their start and end apart: 5, of which 4 were waited for; matrix products, arithmetic and copies ran while one was open for 5% of the time, Pallas kernels for 0%

profile of v1, /device:TPU:0, one launch (start us, length us, event | category | flops | bytes accessed | tf_op | source)
XLA Modules:
  0.0 354.6 jit_solution(9357917484592137796)
XLA Ops:
  10.5 7.3 %all-to-all-start = ((s32[8,1,16]{2,1,0:T(1,128)}), s32[8,1,16]{2,1,0:T(1,128)S(1)}, u32[]{:S(2)}, u32[]{:S(2)}) async-start(s32[8,1,16]{2,1,0:T(1,128)} %bitcast.3), calls=%async_computation | async-start | bytes 8192 | tf_op jit(solution)/shard_map/all_to_all | solution.py:211
  17.8 2.0 copy.135
  22.3 8.8 %all_gather.13 = bf16[409600]{0:T(1024)(128)(2,1)S(1)} all-gather(bf16[102400]{0:T(1024)(128)(2,1)S(1)} %convert_element_type.40), channel_id=1, replica_groups=mesh['node'=4,'edge'=8] {'node'}, dimensions={0}, use_global_device_ids=true | all-gather | bytes 1024000 | tf_op jit(solution)/shard_map/all_gather | solution.py:201
  37.6 27.0 %all-gather.4.cloned.1.call-done = bf16[1024,1152]{1,0:T(8,128)(2,1)} async-done(((bf16[128,1152]{1,0:T(8,128)(2,1)}), bf16[1024,1152]{1,0:T(8,128)(2,1)}) %all-gather.4.cloned.1.call-update) | async-done | bytes 2359312 | tf_op jit(solution)/shard_map/all_gather | solution.py:214
  64.6 3.1 gather_fusion.2
  69.9 68.9 %while.31 = (s32[]{:T(128)}, f32[128,9,128]{2,1,0:T(8,128)}, bf16[512,9,128]{0,2,1:T(8,128)(2,1)}, s32[]{:T(128)}, s32[512]{0:T(512)S(1)}, /*index=5*/f32[64,81]...) while((s32[]{:T(128)}, f32[128,9,128]{2,1,0:T(8,128)}, ...), condition=%wide.region_2.0_spmd.clone, body=%wide.region_0.0_spmd.clone.sunk | while | flops 162342272 | bytes 14705741 | solution.py:250
  80.4 1.9 broadcast_multiply_fusion.5
  97.4 1.9 broadcast_multiply_fusion.5
  114.5 1.9 broadcast_multiply_fusion.5
  150.8 97.3 %while.32 = (s32[]{:T(128)}, f32[128,1152]{1,0:T(8,128)}, f32[384,384]{1,0:T(8,128)}, f32[512,512]{1,0:T(8,128)}, f32[256,256]{1,0:T(8,128)}, /*index=5*/s32[]{:...) while((s32[]{:T(128)}, f32[128,1152]{1,0:T(8,128)}, ...), condition=%wide.region_8.9_spmd.clone, body=%wide.region_6.8_spmd.clone.sunk | while | flops 284963200 | bytes 33641452 | solution.py:279
  164.7 3.6 %scatter_fusion = f32[128,1152]{1,0:T(8,128)} fusion(f32[128,1152]{1,0:T(8,128)} %get-tuple-element.699, s32[128]{0:T(128)S(1)} %compare_select_fusion.7, f32[128,1152]{1,0:T(8,128)S(1)} %copy.228), kind=kCustom, calls=%fused_computation.3.clone.clone.1 | custom fusion | flops 147456 | bytes 1769984 | tf_op jit(solution)/shard_map/while/body/scatter-add | solution.py:265
  170.8 2.6 fusion.151
  188.8 3.6 %scatter_fusion = f32[128,1152]{1,0:T(8,128)} fusion(f32[128,1152]{1,0:T(8,128)} %get-tuple-element.699, s32[128]{0:T(128)S(1)} %compare_select_fusion.7, f32[128,1152]{1,0:T(8,128)S(1)} %copy.228), kind=kCustom, calls=%fused_computation.3.clone.clone.1 | custom fusion | flops 147456 | bytes 1769984 | tf_op jit(solution)/shard_map/while/body/scatter-add | solution.py:265
  194.9 2.6 fusion.151
  212.9 3.6 %scatter_fusion = f32[128,1152]{1,0:T(8,128)} fusion(f32[128,1152]{1,0:T(8,128)} %get-tuple-element.699, s32[128]{0:T(128)S(1)} %compare_select_fusion.7, f32[128,1152]{1,0:T(8,128)S(1)} %copy.228), kind=kCustom, calls=%fused_computation.3.clone.clone.1 | custom fusion | flops 147456 | bytes 1769984 | tf_op jit(solution)/shard_map/while/body/scatter-add | solution.py:265
  219.0 2.6 fusion.151
  237.0 3.6 %scatter_fusion = f32[128,1152]{1,0:T(8,128)} fusion(f32[128,1152]{1,0:T(8,128)} %get-tuple-element.699, s32[128]{0:T(128)S(1)} %compare_select_fusion.7, f32[128,1152]{1,0:T(8,128)S(1)} %copy.228), kind=kCustom, calls=%fused_computation.3.clone.clone.1 | custom fusion | flops 147456 | bytes 1769984 | tf_op jit(solution)/shard_map/while/body/scatter-add | solution.py:265
  243.1 2.6 fusion.151
  258.6 32.6 %all-reduce.3.cloned.1.call-done = bf16[409600]{0:T(1024)(128)(2,1)} async-done(((bf16[409600]{0:T(1024)(128)(2,1)}), bf16[409600]{0:T(1024)(128)(2,1)}) %all-reduce.3.cloned.1.call-update) | async-done | bytes 819216
  292.8 5.7 %all-to-all-start.1 = ((f32[8,16,1152]{2,1,0:T(8,128)}), f32[8,16,1152]{2,1,0:T(8,128)S(1)}, u32[]{:S(2)}, u32[]{:S(2)}) async-start(f32[8,16,1152]{2,1,0:T(8,128)} %bitcast.17), calls=%async_computation.1 | async-start | bytes 1179648 | tf_op jit(solution)/shard_map/all_to_all | solution.py:280
  300.8 19.1 %all-to-all-done.1 = f32[8,16,1152]{2,1,0:T(8,128)S(1)} async-done(((f32[8,16,1152]{2,1,0:T(8,128)}), f32[8,16,1152]{2,1,0:T(8,128)S(1)}, u32[]{:S(2)}, u32[]{:S(2)}) %all-to-all-start.1) | async-done | bytes 589856 | tf_op jit(solution)/shard_map/all_to_all | solution.py:280
  319.9 2.0 scatter_fusion.1
  322.7 20.8 %all-gather.6.cloned.1.call-done = bf16[819200]{0:T(1024)(128)(2,1)} async-done(((bf16[102400]{0:T(1024)(128)(2,1)}), bf16[819200]{0:T(1024)(128)(2,1)}) %all-gather.6.cloned.1.call-update) | async-done | bytes 1638416 | tf_op jit(solution)/shard_map/all_gather | solution.py:296
  343.4 2.1 reshape.398
  (480 shorter events, 170.1 us)
Async XLA Ops:
  7.2 26.3 %copy-start = (f32[64,9,9]{0,2,1:T(8,128)S(1)}, f32[64,9,9]{0,2,1:T(8,128)}, u32[]{:S(2)}) copy-start(f32[64,9,9]{0,2,1:T(8,128)} %param.26) | copy-start | bytes 62212
  7.2 13.7 %copy-start.27 = (bf16[128,1152]{1,0:T(8,128)(2,1)S(1)}, bf16[128,1152]{1,0:T(8,128)(2,1)}, u32[]{:S(2)}) copy-start(bf16[128,1152]{1,0:T(8,128)(2,1)} %param.19) | copy-start | bytes 884740
  7.2 14.8 %copy-start.34 = (s32[128,4]{0,1:T(4,128)S(1)}, s32[128,4]{0,1:T(4,128)}, u32[]{:S(2)}) copy-start(s32[128,4]{0,1:T(4,128)} %param.25) | copy-start | bytes 6148
  7.2 15.0 %copy-start.25 = (f32[102400]{0:T(1024)S(1)}, f32[102400]{0:T(1024)}, u32[]{:S(2)}) copy-start(f32[102400]{0:T(1024)} %param.20) | copy-start | bytes 1228804
  7.2 57.4 %all-gather.4.cloned.1.call-start = ((), (), s32[]{:S(2)}) async-start(), calls=%async_computation.2 | async-start | bytes 2654208 | tf_op jit(solution)/shard_map/all_gather | solution.py:214
  10.5 26.4 %all-to-all-start = ((s32[8,1,16]{2,1,0:T(1,128)}), s32[8,1,16]{2,1,0:T(1,128)S(1)}, u32[]{:S(2)}, u32[]{:S(2)}) async-start(s32[8,1,16]{2,1,0:T(1,128)} %bitcast.3), calls=%async_computation | async-start | bytes 8192 | tf_op jit(solution)/shard_map/all_to_all | solution.py:211
  17.7 273.4 %all-reduce.3.cloned.1.call-start = ((), (), s32[]{:S(2)}) async-start(), calls=%async_computation.4 | async-start | bytes 1638400
  20.9 11.1 %copy-start.23 = (bf16[128,1152]{0,1:T(8,128)(2,1)}, bf16[128,1152]{0,1:T(8,128)(2,1)S(1)}, u32[]{:S(2)}) copy-start(bf16[128,1152]{0,1:T(8,128)(2,1)S(1)} %copy.144) | copy-start | bytes 884740
  22.2 9.1 %copy-start.39 = (s32[9]{0:T(128)S(1)}, s32[9]{0:T(128)}, u32[]{:S(2)}) copy-start(s32[9]{0:T(128)} %constant.135) | copy-start | bytes 112
  70.5 6.7 %copy-start.3 = (bf16[384,384]{1,0:T(8,128)(2,1)}, bf16[384,384]{1,0:T(8,128)(2,1)S(1)}, u32[]{:S(2)}) copy-start(bf16[384,384]{1,0:T(8,128)(2,1)S(1)} %get-tuple-element.667) | copy-start | bytes 884740 | tf_op jit(solution)/shard_map/while
  87.6 6.7 %copy-start.3 = (bf16[384,384]{1,0:T(8,128)(2,1)}, bf16[384,384]{1,0:T(8,128)(2,1)S(1)}, u32[]{:S(2)}) copy-start(bf16[384,384]{1,0:T(8,128)(2,1)S(1)} %get-tuple-element.667) | copy-start | bytes 884740 | tf_op jit(solution)/shard_map/while
  151.7 8.0 %copy-start.1 = (bf16[512,512]{1,0:T(8,128)(2,1)}, bf16[512,512]{1,0:T(8,128)(2,1)S(1)}, u32[]{:S(2)}) copy-start(bf16[512,512]{1,0:T(8,128)(2,1)S(1)} %get-tuple-element.732) | copy-start | bytes 1572868 | tf_op jit(solution)/shard_map/while
  151.7 9.2 %copy-start.5 = (bf16[384,384]{1,0:T(8,128)(2,1)}, bf16[384,384]{1,0:T(8,128)(2,1)S(1)}, u32[]{:S(2)}) copy-start(bf16[384,384]{1,0:T(8,128)(2,1)S(1)} %get-tuple-element.731) | copy-start | bytes 884740 | tf_op jit(solution)/shard_map/while
  175.8 8.0 %copy-start.1 = (bf16[512,512]{1,0:T(8,128)(2,1)}, bf16[512,512]{1,0:T(8,128)(2,1)S(1)}, u32[]{:S(2)}) copy-start(bf16[512,512]{1,0:T(8,128)(2,1)S(1)} %get-tuple-element.732) | copy-start | bytes 1572868 | tf_op jit(solution)/shard_map/while
  175.8 9.2 %copy-start.5 = (bf16[384,384]{1,0:T(8,128)(2,1)}, bf16[384,384]{1,0:T(8,128)(2,1)S(1)}, u32[]{:S(2)}) copy-start(bf16[384,384]{1,0:T(8,128)(2,1)S(1)} %get-tuple-element.731) | copy-start | bytes 884740 | tf_op jit(solution)/shard_map/while
  199.9 8.0 %copy-start.1 = (bf16[512,512]{1,0:T(8,128)(2,1)}, bf16[512,512]{1,0:T(8,128)(2,1)S(1)}, u32[]{:S(2)}) copy-start(bf16[512,512]{1,0:T(8,128)(2,1)S(1)} %get-tuple-element.732) | copy-start | bytes 1572868 | tf_op jit(solution)/shard_map/while
  199.9 9.2 %copy-start.5 = (bf16[384,384]{1,0:T(8,128)(2,1)}, bf16[384,384]{1,0:T(8,128)(2,1)S(1)}, u32[]{:S(2)}) copy-start(bf16[384,384]{1,0:T(8,128)(2,1)S(1)} %get-tuple-element.731) | copy-start | bytes 884740 | tf_op jit(solution)/shard_map/while
  224.0 8.0 %copy-start.1 = (bf16[512,512]{1,0:T(8,128)(2,1)}, bf16[512,512]{1,0:T(8,128)(2,1)S(1)}, u32[]{:S(2)}) copy-start(bf16[512,512]{1,0:T(8,128)(2,1)S(1)} %get-tuple-element.732) | copy-start | bytes 1572868 | tf_op jit(solution)/shard_map/while
  224.0 9.2 %copy-start.5 = (bf16[384,384]{1,0:T(8,128)(2,1)}, bf16[384,384]{1,0:T(8,128)(2,1)S(1)}, u32[]{:S(2)}) copy-start(bf16[384,384]{1,0:T(8,128)(2,1)S(1)} %get-tuple-element.731) | copy-start | bytes 884740 | tf_op jit(solution)/shard_map/while
  257.2 41.2 %copy-start.40 = (s32[1,1,128]{2,1,0:T(1,128)S(1)}, s32[1,1,128]{2,1,0:T(1,128)}, u32[]{:S(2)}) copy-start(s32[1,1,128]{2,1,0:T(1,128)} %param.23) | copy-start | bytes 1540
  257.2 41.3 %copy-start.15 = (f32[128,9,128]{0,2,1:T(8,128)S(1)}, f32[128,9,128]{0,2,1:T(8,128)}, u32[]{:S(2)}) copy-start(f32[128,9,128]{0,2,1:T(8,128)} %copy-done.14) | copy-start | bytes 1769476
  257.3 86.2 %all-gather.6.cloned.1.call-start = ((), (), s32[]{:S(2)}) async-start(), calls=%async_computation.3 | async-start | bytes 1843200 | tf_op jit(solution)/shard_map/all_gather | solution.py:296
  292.8 7.8 %copy-start.20 = (f32[128,9,128]{0,2,1:T(8,128)S(1)}, f32[128,9,128]{0,2,1:T(8,128)}, u32[]{:S(2)}) copy-start(f32[128,9,128]{0,2,1:T(8,128)} %copy-done.19) | copy-start | bytes 1769476
  292.8 27.1 %all-to-all-start.1 = ((f32[8,16,1152]{2,1,0:T(8,128)}), f32[8,16,1152]{2,1,0:T(8,128)S(1)}, u32[]{:S(2)}, u32[]{:S(2)}) async-start(f32[8,16,1152]{2,1,0:T(8,128)} %bitcast.17), calls=%async_computation.1 | async-start | bytes 1179648 | tf_op jit(solution)/shard_map/all_to_all | solution.py:280
  (71 other events, 213.7 us)
Sparse Core Ops, SparseCore 0:
  10.2 54.3 all-gather.3
  257.4 33.7 all-reduce.2
  293.9 49.4 all-gather.5
